TPU v7x, 128 devices: a whole 4x4x4 slice. The times are simulated.
128 devices in a mesh: chan: 16 (over y_lo, z, core), tile: 8 (over y_hi, x).
Axes of the slice: x: 4, y: 4 (y_hi: 2, y_lo: 2; y = y_hi * 2 + y_lo), z: 4, core: 2. Of those that a mesh axis runs over, the one named last changes fastest.
Arguments:
- voltages: bfloat16 [524288, 2048], P('chan', 'tile'), may hold values from -4 to 4
- pfb_taps: float32 [4, 2048], replicated, may hold values from -3 to 3
Outputs:
- visibility: float32 [32, 2, 2048, 2048], P('chan', None, 'tile')
All inputs are finite; a program needn't handle non-finite values.
Results may differ from a plain program's by a relative error of at most 0.0038.
Values may be sent and summed in bfloat16 or wider, within the bound.
A program may use at most 192 MiB of HBM per device.

v0:
```python
import math

import jax
import jax.numpy as jnp
from jax import lax
from jax.sharding import PartitionSpec as P

CH_DEV = 2


def from_behind(block, axis, distance):
    devices = range(lax.axis_size(axis))
    route = [(i - distance, i) for i in devices if i - distance in devices]
    return lax.ppermute(block, axis, route)


def dft_table(frame_len, channel_count):
    samples = jnp.arange(frame_len, dtype=jnp.int32)
    centers = frame_len // 8 + jnp.arange(channel_count, dtype=jnp.int32)
    phase_index = samples[:, None] * centers[None, :] % frame_len
    angle = 2.0 * jnp.pi / frame_len * phase_index.astype(jnp.float32)
    factor = 1.0 / math.sqrt(frame_len)
    return jnp.concatenate([jnp.cos(angle) * factor, -jnp.sin(angle) * factor], axis=1)


def filter_frames(pfb_taps, extended, count):
    total = pfb_taps[0][:, None] * extended[0:count]
    for tap_index in range(1, pfb_taps.shape[0]):
        total = total + pfb_taps[tap_index][:, None] * extended[tap_index : tap_index + count]
    return total


def channelize(table, pfb_taps, samples, count, block):
    tap_count = pfb_taps.shape[0]
    frame_len = pfb_taps.shape[1]
    inputs_here = samples.shape[1]

    def one_block(block_index):
        window = lax.dynamic_slice_in_dim(
            samples, block_index * block * frame_len, (block + tap_count - 1) * frame_len, 0
        )
        frames = window.astype(jnp.float32).reshape(block + tap_count - 1, frame_len, inputs_here)
        filtered = filter_frames(pfb_taps, frames, block)
        return jnp.einsum(
            "nc,sni->sci",
            table,
            filtered,
            precision=lax.Precision.HIGHEST,
            preferred_element_type=jnp.float32,
        )

    result = lax.map(one_block, jnp.arange(count // block, dtype=jnp.int32))
    return result.reshape(count, result.shape[2], inputs_here)


def shards(voltages, pfb_taps):
    chan_count = lax.axis_size("chan")
    tap_count = pfb_taps.shape[0]
    frame_len = pfb_taps.shape[1]
    inputs_here = voltages.shape[1]
    spec_here = voltages.shape[0] // frame_len
    overhang = tap_count - 1
    channels = CH_DEV * chan_count
    table = dft_table(frame_len, channels)
    leading = voltages[: overhang * frame_len]
    arrived = from_behind(leading, "chan", -1)
    extended = jnp.concatenate([voltages, arrived], axis=0)
    spectra = channelize(table, pfb_taps, extended, spec_here, 4)
    spectra = spectra.astype(jnp.bfloat16).reshape(spec_here, 2, channels, inputs_here)
    turned = lax.all_to_all(spectra, "chan", split_axis=2, concat_axis=0, tiled=True)
    total_spectra = turned.shape[0]
    products = jnp.einsum(
        "sacp,sbcq->capbq",
        turned,
        lax.all_gather(turned, "tile", axis=3, tiled=True),
        preferred_element_type=jnp.float32,
    )
    real_part = products[:, 0, :, 0, :] + products[:, 1, :, 1, :]
    imag_part = products[:, 1, :, 0, :] - products[:, 0, :, 1, :]
    return jnp.stack([real_part, imag_part], axis=1) / total_spectra


def solution(mesh):
    placed = (P("chan", "tile"), P())
    return jax.shard_map(
        shards, mesh=mesh, in_specs=placed, out_specs=P("chan", None, "tile", None), check_vma=False
    )
```

profile of v0, /device:TPU:0, one launch (start us, length us, event | category | flops | bytes accessed | tf_op | source)
XLA Modules:
  0.0 355.2 jit_solution(6156543650741576212)
XLA Ops:
  6.5 3.8 %slice.75 = bf16[6144,256]{1,0:T(8,128)(2,1)} slice(bf16[32768,256]{1,0:T(8,128)(2,1)} %param.4), slice={[0:6144], [0:256]} | slice | bytes 6291456 | tf_op jit(solution)/shard_map/slice | solution.py:65
  10.3 1.3 collective-permute-start
  11.6 1.1 cosine_multiply_fusion
  12.8 5.4 %collective-permute-done = bf16[6144,256]{1,0:T(8,128)(2,1)} collective-permute-done((bf16[6144,256]{1,0:T(8,128)(2,1)}, bf16[6144,256]{1,0:T(8,128)(2,1)}, u32[]{:S(2)}, u32[]{:S(2)}) %collective-permute-start) | collective-permute-done | bytes 3145760 | tf_op jit(solution)/shard_map/ppermute | solution.py:14
  18.2 20.0 %pad_maximum_fusion = bf16[38912,256]{1,0:T(8,128)(2,1)} fusion(bf16[6144,256]{1,0:T(8,128)(2,1)} %collective-permute-done, bf16[32768,256]{1,0:T(8,128)(2,1)} %param.4), kind=kLoop, calls=%fused_computation.16 | loop fusion | flops 39845888 | bytes 39845888 | tf_op jit(solution)/shard_map/concatenate | solution.py:67
  38.2 170.7 %while.12 = (s32[]{:T(128)}, bf16[4,4,64,256]{3,2,1,0:T(8,128)(2,1)S(1)}, f32[4,2048]{1,0:T(4,128)S(1)}, s32[4]{0:T(128)S(1)}, bf16[38912,256]{1,0:T(8,128)(2,1)...) while((s32[]{:T(128)}, bf16[4,4,64,256]{3,2,1,0:T(8,128)(2,1)S(1)}, ...), condition=%wide.region_1.2_spmd, body=%wide.region_0.1_spmd.sunk | while | flops 1628962816 | bytes 123568296 | solution.py:52
  38.2 0.6 dynamic_slice.17
  39.4 8.2 %dynamic-slice_convert_fusion.2 = f32[14336,256]{1,0:T(8,128)} fusion(bf16[38912,256]{1,0:T(8,128)(2,1)} %get-tuple-element.182, s32[]{:T(128)S(6)} %select_n.26), kind=kLoop, calls=%fused_computation.8.clone.1 | loop fusion | flops 3670016 | bytes 22020100 | tf_op jit(solution)/shard_map/while/body/eval_jaxpr/convert_element_type | solution.py:42
  47.7 20.9 %fusion.40 = (f32[8192,256]{1,0:T(8,128)S(1)}, f32[8192,256]{1,0:T(8,128)}, f32[8192,256]{1,0:T(8,128)}, f32[8192,256]{1,0:T(8,128)}) fusion(f32[14336,256]{1,0:T(8,128)} %dynamic-slice_convert_fusion.2), kind=kLoop, calls=%fused_computation.39.clone.1 | loop fusion | bytes 67108864 | tf_op jit(solution)/shard_map/while/body/eval_jaxpr/slice | solution.py:27
  68.7 12.2 %fusion.42 = bf16[4,4,64,256]{3,2,1,0:T(8,128)(2,1)S(1)} fusion(bf16[4,4,64,256]{3,2,1,0:T(8,128)(2,1)S(1)} %get-tuple-element.169, s32[]{:T(128)} %get-tuple-element.168, f32[4,2048,256]{2,1,0:T(8,128)} %bitcast.70, f32[4,2048,256]{2,1,0:T(8,128)} %bitcast.71, f32[4,2048,256]{2,1,0:T(8,128)} %bitcast.72, f32[4,2048,256]{2,1,0:T(8,128)S(1)} %bitcast.69, ...), kind=kOutput, calls=%fused_computation.14.clone.1 | convolution fusion | flops 1625292800 | bytes 34373636 | tf_op jit(solution)/shard_map/while/body/eval_jaxpr/nc,sni->sci/dot_general | solution.py:44
  80.9 0.6 dynamic_slice.17
  82.1 8.2 %dynamic-slice_convert_fusion.2 = f32[14336,256]{1,0:T(8,128)} fusion(bf16[38912,256]{1,0:T(8,128)(2,1)} %get-tuple-element.182, s32[]{:T(128)S(6)} %select_n.26), kind=kLoop, calls=%fused_computation.8.clone.1 | loop fusion | flops 3670016 | bytes 22020100 | tf_op jit(solution)/shard_map/while/body/eval_jaxpr/convert_element_type | solution.py:42
  90.4 20.9 %fusion.40 = (f32[8192,256]{1,0:T(8,128)S(1)}, f32[8192,256]{1,0:T(8,128)}, f32[8192,256]{1,0:T(8,128)}, f32[8192,256]{1,0:T(8,128)}) fusion(f32[14336,256]{1,0:T(8,128)} %dynamic-slice_convert_fusion.2), kind=kLoop, calls=%fused_computation.39.clone.1 | loop fusion | bytes 67108864 | tf_op jit(solution)/shard_map/while/body/eval_jaxpr/slice | solution.py:27
  111.3 12.2 %fusion.42 = bf16[4,4,64,256]{3,2,1,0:T(8,128)(2,1)S(1)} fusion(bf16[4,4,64,256]{3,2,1,0:T(8,128)(2,1)S(1)} %get-tuple-element.169, s32[]{:T(128)} %get-tuple-element.168, f32[4,2048,256]{2,1,0:T(8,128)} %bitcast.70, f32[4,2048,256]{2,1,0:T(8,128)} %bitcast.71, f32[4,2048,256]{2,1,0:T(8,128)} %bitcast.72, f32[4,2048,256]{2,1,0:T(8,128)S(1)} %bitcast.69, ...), kind=kOutput, calls=%fused_computation.14.clone.1 | convolution fusion | flops 1625292800 | bytes 34373636 | tf_op jit(solution)/shard_map/while/body/eval_jaxpr/nc,sni->sci/dot_general | solution.py:44
  123.6 0.6 dynamic_slice.17
  124.8 8.2 %dynamic-slice_convert_fusion.2 = f32[14336,256]{1,0:T(8,128)} fusion(bf16[38912,256]{1,0:T(8,128)(2,1)} %get-tuple-element.182, s32[]{:T(128)S(6)} %select_n.26), kind=kLoop, calls=%fused_computation.8.clone.1 | loop fusion | flops 3670016 | bytes 22020100 | tf_op jit(solution)/shard_map/while/body/eval_jaxpr/convert_element_type | solution.py:42
  133.1 20.9 %fusion.40 = (f32[8192,256]{1,0:T(8,128)S(1)}, f32[8192,256]{1,0:T(8,128)}, f32[8192,256]{1,0:T(8,128)}, f32[8192,256]{1,0:T(8,128)}) fusion(f32[14336,256]{1,0:T(8,128)} %dynamic-slice_convert_fusion.2), kind=kLoop, calls=%fused_computation.39.clone.1 | loop fusion | bytes 67108864 | tf_op jit(solution)/shard_map/while/body/eval_jaxpr/slice | solution.py:27
  154.0 12.2 %fusion.42 = bf16[4,4,64,256]{3,2,1,0:T(8,128)(2,1)S(1)} fusion(bf16[4,4,64,256]{3,2,1,0:T(8,128)(2,1)S(1)} %get-tuple-element.169, s32[]{:T(128)} %get-tuple-element.168, f32[4,2048,256]{2,1,0:T(8,128)} %bitcast.70, f32[4,2048,256]{2,1,0:T(8,128)} %bitcast.71, f32[4,2048,256]{2,1,0:T(8,128)} %bitcast.72, f32[4,2048,256]{2,1,0:T(8,128)S(1)} %bitcast.69, ...), kind=kOutput, calls=%fused_computation.14.clone.1 | convolution fusion | flops 1625292800 | bytes 34373636 | tf_op jit(solution)/shard_map/while/body/eval_jaxpr/nc,sni->sci/dot_general | solution.py:44
  166.2 0.6 dynamic_slice.17
  167.5 8.2 %dynamic-slice_convert_fusion.2 = f32[14336,256]{1,0:T(8,128)} fusion(bf16[38912,256]{1,0:T(8,128)(2,1)} %get-tuple-element.182, s32[]{:T(128)S(6)} %select_n.26), kind=kLoop, calls=%fused_computation.8.clone.1 | loop fusion | flops 3670016 | bytes 22020100 | tf_op jit(solution)/shard_map/while/body/eval_jaxpr/convert_element_type | solution.py:42
  175.7 20.9 %fusion.40 = (f32[8192,256]{1,0:T(8,128)S(1)}, f32[8192,256]{1,0:T(8,128)}, f32[8192,256]{1,0:T(8,128)}, f32[8192,256]{1,0:T(8,128)}) fusion(f32[14336,256]{1,0:T(8,128)} %dynamic-slice_convert_fusion.2), kind=kLoop, calls=%fused_computation.39.clone.1 | loop fusion | bytes 67108864 | tf_op jit(solution)/shard_map/while/body/eval_jaxpr/slice | solution.py:27
  196.7 12.2 %fusion.42 = bf16[4,4,64,256]{3,2,1,0:T(8,128)(2,1)S(1)} fusion(bf16[4,4,64,256]{3,2,1,0:T(8,128)(2,1)S(1)} %get-tuple-element.169, s32[]{:T(128)} %get-tuple-element.168, f32[4,2048,256]{2,1,0:T(8,128)} %bitcast.70, f32[4,2048,256]{2,1,0:T(8,128)} %bitcast.71, f32[4,2048,256]{2,1,0:T(8,128)} %bitcast.72, f32[4,2048,256]{2,1,0:T(8,128)S(1)} %bitcast.69, ...), kind=kOutput, calls=%fused_computation.14.clone.1 | convolution fusion | flops 1625292800 | bytes 34373636 | tf_op jit(solution)/shard_map/while/body/eval_jaxpr/nc,sni->sci/dot_general | solution.py:44
  208.9 0.3 copy.19
  209.2 48.7 %all_to_all.18 = bf16[16,2,32,256]{3,0,1,2:T(8,128)(2,1)S(1)} all-to-all(bf16[16,2,32,256]{3,0,1,2:T(8,128)(2,1)S(1)} %copy.19), channel_id=1, replica_groups=mesh['chan'=16,'tile'=8] {'chan'}, dimensions={2} | all-to-all | bytes 1048576 | tf_op jit(solution)/shard_map/all_to_all | solution.py:70
  258.0 0.8 copy.21
  258.8 0.0 all-gather.2.cloned.1.call-update
  258.8 77.6 %all-gather.2.cloned.1.call-done = bf16[256,2,2,2048]{3,0,1,2:T(8,128)(2,1)} async-done(((bf16[256,2,2,256]{3,0,1,2:T(8,128)(2,1)}), bf16[256,2,2,2048]{3,0,1,2:T(8,128)(2,1)}) %all-gather.2.cloned.1.call-update) | async-done | bytes 4194320 | tf_op jit(solution)/shard_map/all_gather | solution.py:75
  336.4 4.7 %fusion.22 = f32[2,2,256,2,2048]{4,2,3,1,0:T(8,128)S(1)} fusion(bf16[256,2,2,256,1]{3,0,4,1,2:T(8,128)(2,1)} %bitcast.74, bf16[256,2,2,2048]{3,0,1,2:T(8,128)(2,1)} %all-gather.2.cloned.1.call-done), kind=kOutput, calls=%fused_computation.24 | convolution fusion | flops 2147483648 | bytes 21495808 | tf_op jit(solution)/shard_map/sacp,sbcq->capbq/dot_general | solution.py:72
  341.1 0.8 fusion.19
  341.9 0.8 fusion.21
  342.7 1.6 maximum_multiply_fusion
  344.3 4.0 %copy.25 = f32[2,2,256,2048]{3,2,1,0:T(8,128)} copy(f32[2,2,256,2048]{3,2,0,1:T(8,128)S(1)} %maximum_multiply_fusion) | data formatting | bytes 16777216 | tf_op jit(solution)/shard_map/div | solution.py:80
  (11 shorter events, 0.1 us)
Async XLA Ops:
  6.5 329.9 %all-gather.2.cloned.1.call-start = ((), (), s32[]{:S(2)}) async-start(), calls=%async_computation.1 | async-start | bytes 4718592 | tf_op jit(solution)/shard_map/all_gather | solution.py:75
  10.3 7.9 %collective-permute-start = (bf16[6144,256]{1,0:T(8,128)(2,1)}, bf16[6144,256]{1,0:T(8,128)(2,1)}, u32[]{:S(2)}, u32[]{:S(2)}) collective-permute-start(bf16[6144,256]{1,0:T(8,128)(2,1)} %slice.75), channel_id=1, source_target_pairs={{8,0},{16,8},{24,16},{32,24},{40,32},{48,40},{56,48},{64,56},{72,6... | collective-permute-start | bytes 9437192 | tf_op jit(solution)/shard_map/ppermute | solution.py:14
  12.8 25.4 %copy-start = (f32[4,2048]{1,0:T(4,128)S(1)}, f32[4,2048]{1,0:T(4,128)}, u32[]{:S(2)}) copy-start(f32[4,2048]{1,0:T(4,128)} %param.5) | copy-start | bytes 98308
Sparse Core Ops, SparseCore 0:
  258.9 77.4 all-gather.1
where the time goes:
time: 356 us; the launch traced here: 355 us
  local copies, waits for them, and re-layouts  95.1 us (27%)
  waiting for transfers between devices  83 us (23%)
  other arithmetic  57.3 us (16%)
  matrix products  53.5 us (15%)
  blocking collectives  48.7 us (14%)
  between operations  13.5 us (4%)
    slice x8, local copies, waits for them, and re-layouts, filter_frames(): total = pfb_taps[0][:, None] * extended[0:count]  83.9 us
    all_gather x1, waiting for transfers between devices, shards(): lax.all_gather(turned, 'tile', axis=3, tiled=True)  77.6 us
    dot_general x4, matrix products, one_block(): jnp.einsum('nc,sni->sci', table, filtered, precision=lax.Precision.HIGHES...  48.8 us
    all_to_all x1, blocking collectives, shards(): lax.all_to_all(spectra, 'chan', split_axis=2, concat_axis=0, tiled=True)  48.7 us
    convert_element_type x4, other arithmetic, one_block(): window.astype(jnp.float32)  33 us
    concatenate x1, other arithmetic, shards(): extended = jnp.concatenate([voltages, arrived], axis=0)  20 us
  transfers between devices with their start and end apart: 2, of which 2 were waited for; matrix products, arithmetic and copies ran while one was open for 0% of the time, Pallas kernels for 0%

commit v1 on v0

v1 whole, which is shorter than its diff:
```python
import functools
import math

import jax
import jax.numpy as jnp
import numpy as np
from jax import lax
from jax.experimental import pallas as pl
from jax.experimental.pallas import tpu as pltpu
from jax.sharding import PartitionSpec as P

FFT = 2048
TAPS = 4
CHANNELS = 32
ROWS = 2 * CHANNELS
HALO = TAPS - 1


def dft_rows():
    samples = np.arange(FFT, dtype=np.int64)
    centers = FFT // 8 + np.arange(CHANNELS, dtype=np.int64)
    angle = 2.0 * np.pi / FFT * (centers[:, None] * samples[None, :] % FFT)
    factor = 1.0 / math.sqrt(FFT)
    return np.concatenate([np.cos(angle), -np.sin(angle)], axis=0).astype(np.float32) * np.float32(factor)


def channelize_kernel(taps_ref, table_ref, frame_ref, done_ref, tail_ref, head_ref, weights, sums):
    f = pl.program_id(0)
    last = pl.num_programs(0) - 1

    @pl.when(f == 0)
    def _():
        for t in range(TAPS):
            full = taps_ref[t : t + 1, :] * table_ref[...]
            high = full.astype(jnp.bfloat16)
            weights[2 * t * ROWS : (2 * t + 1) * ROWS, :] = high
            weights[(2 * t + 1) * ROWS : (2 * t + 2) * ROWS, :] = (full - high.astype(jnp.float32)).astype(jnp.bfloat16)
        sums[0 : HALO * ROWS, :] = jnp.zeros((HALO * ROWS, sums.shape[1]), jnp.float32)

    part = jnp.dot(weights[...], frame_ref[...], preferred_element_type=jnp.float32)
    for t in range(TAPS):
        term = part[2 * t * ROWS : (2 * t + 1) * ROWS] + part[(2 * t + 1) * ROWS : (2 * t + 2) * ROWS]
        at = pl.ds(pl.multiple_of((f + HALO - t) * ROWS, ROWS), ROWS)
        if t == 0:
            sums[at, :] = term
        else:
            sums[at, :] += term

    @pl.when(f == last)
    def _():
        count = pl.num_programs(0)
        head_ref[...] = sums[0 : HALO * ROWS, :]
        tail_ref[...] = sums[16 * ROWS : 19 * ROWS, :]
        done_ref[...] = sums[HALO * ROWS : 16 * ROWS, :].astype(jnp.bfloat16)


def channelize(pfb_taps, voltages):
    inputs = voltages.shape[1]
    frames = voltages.shape[0] // FFT
    full = lambda shape: pl.BlockSpec(shape, lambda f: (0, 0))
    return pl.pallas_call(
        channelize_kernel,
        grid=(frames,),
        in_specs=[full((TAPS, FFT)), full((ROWS, FFT)), pl.BlockSpec((FFT, inputs), lambda f: (f, 0))],
        out_specs=[full(((frames - HALO) * ROWS, inputs)), full((HALO * ROWS, inputs)), full((HALO * ROWS, inputs))],
        out_shape=[
            jax.ShapeDtypeStruct(((frames - HALO) * ROWS, inputs), jnp.bfloat16),
            jax.ShapeDtypeStruct((HALO * ROWS, inputs), jnp.float32),
            jax.ShapeDtypeStruct((HALO * ROWS, inputs), jnp.float32),
        ],
        scratch_shapes=[
            pltpu.VMEM((2 * TAPS * ROWS, FFT), jnp.bfloat16),
            pltpu.VMEM(((frames + HALO) * ROWS, inputs), jnp.float32),
        ],
        compiler_params=pltpu.CompilerParams(vmem_limit_bytes=40 << 20),
    )(pfb_taps, dft_rows(), voltages)


def correlate_kernel(scale, own_ref, other_ref, out_ref, left):
    half = own_ref.shape[1] // 2

    @pl.when(pl.program_id(1) == 0)
    def _():
        own = own_ref[0].astype(jnp.float32).T
        left[0:256, :] = own.astype(jnp.bfloat16)
        left[256:512, :] = jnp.concatenate([own[:, half:], -own[:, :half]], axis=1).astype(jnp.bfloat16)

    for q in range(other_ref.shape[0]):
        block = jnp.dot(left[...], other_ref[q, 0], preferred_element_type=jnp.float32) * scale
        out_ref[0, 0, :, q * 256 : (q + 1) * 256] = block[:256]
        out_ref[0, 1, :, q * 256 : (q + 1) * 256] = block[256:]


def correlate(own, gathered, spectra):
    tiles, channels, depth, inputs = gathered.shape
    step = 2
    return pl.pallas_call(
        functools.partial(correlate_kernel, 1.0 / spectra),
        grid=(channels, tiles // step),
        in_specs=[
            pl.BlockSpec((1, depth, inputs), lambda c, q: (c, 0, 0)),
            pl.BlockSpec((step, 1, depth, inputs), lambda c, q: (q, c, 0, 0)),
        ],
        out_specs=pl.BlockSpec((1, 2, inputs, step * inputs), lambda c, q: (c, 0, 0, q)),
        out_shape=jax.ShapeDtypeStruct((channels, 2, inputs, tiles * inputs), jnp.float32),
        scratch_shapes=[pltpu.VMEM((2 * inputs, depth), jnp.bfloat16)],
        compiler_params=pltpu.CompilerParams(vmem_limit_bytes=40 << 20),
    )(own, gathered)


def shards(voltages, pfb_taps):
    chans = lax.axis_size("chan")
    frames = voltages.shape[0] // FFT
    inputs = voltages.shape[1]
    done, tail, head = channelize(pfb_taps, voltages)
    arrived = lax.ppermute(head, "chan", [(i + 1, i) for i in range(chans - 1)])
    ending = (tail + arrived).astype(jnp.bfloat16)
    spectra = jnp.concatenate([done, ending], axis=0).reshape(frames, 2, chans, CHANNELS // chans, inputs)
    spectra = spectra.transpose(2, 3, 1, 0, 4)
    turned = lax.all_to_all(spectra, "chan", split_axis=0, concat_axis=0, tiled=True)
    own = turned.transpose(1, 2, 0, 3, 4).reshape(CHANNELS // chans, 2 * chans * frames, inputs)
    gathered = lax.all_gather(own, "tile", axis=0, tiled=False)
    return correlate(own, gathered, chans * frames)


def solution(mesh):
    placed = (P("chan", "tile"), P())
    return jax.shard_map(
        shards, mesh=mesh, in_specs=placed, out_specs=P("chan", None, "tile", None), check_vma=False
    )
```

time: 356 us -> 140 us (0.39)
  local copies, waits for them, and re-layouts: 95.1 us -> 6.35 us
  other arithmetic: 57.3 us -> 0.06 us
  matrix products: 53.5 us -> 0 us
  blocking collectives: 48.7 us -> 21.4 us
  Pallas kernels: 0 us -> 23.9 us
  waiting for transfers between devices: 83 us -> 73 us
    slice x9 -> x0, local copies, waits for them, and re-layouts: 87.6 us -> none  [the longest x8 83.9 us: filter_frames(): total = pfb_taps[0][:, None] * extended[0:count]]
    dot_general x5 -> x0, matrix products: 53.5 us -> none  [the longest x4 48.8 us: one_block(): jnp.einsum('nc,sni->sci', table, filtered, precision=lax.Precision.HIGHES...]
    convert_element_type x4 -> x1, other arithmetic: 33 us -> 0.02 us  [shards(): ending = (tail + arrived).astype(jnp.bfloat16)]
    all_to_all x1, blocking collectives: 48.7 us -> 21.4 us  [shards(): lax.all_to_all(spectra, 'chan', split_axis=0, concat_axis=0, tiled=True)]
    pallas_call x0 -> x2, Pallas kernels: none -> 23.9 us  [the longest x1 17.3 us: channelize(): pl.pallas_call(channelize_kernel, grid=(frames,), in_specs=[full((TAPS, F...]
    concatenate x2 -> x1, other arithmetic: 20 us -> 0.04 us  [shards(): jnp.concatenate([done, ending], axis=0)]
    all_gather x1, waiting for transfers between devices: 77.6 us -> 71 us  [shards(): gathered = lax.all_gather(own, 'tile', axis=0, tiled=False)]
    unnamed x2 -> x8, local copies, waits for them, and re-layouts: 0.01 us -> 5.03 us
where the time goes in v1:
time: 140 us; the launch traced here: 139 us
  waiting for transfers between devices  73 us (52%)
  Pallas kernels  23.9 us (17%)
  blocking collectives  21.4 us (15%)
  between operations  13.4 us (10%)
  local copies, waits for them, and re-layouts  6.35 us (5%)
    all_gather x1, waiting for transfers between devices, shards(): gathered = lax.all_gather(own, 'tile', axis=0, tiled=False)  71 us
    all_to_all x1, blocking collectives, shards(): lax.all_to_all(spectra, 'chan', split_axis=0, concat_axis=0, tiled=True)  21.4 us
    pallas_call x1, Pallas kernels, channelize(): pl.pallas_call(channelize_kernel, grid=(frames,), in_specs=[full((TAPS, F...  17.3 us
    pallas_call x1, Pallas kernels, correlate(): pl.pallas_call(functools.partial(correlate_kernel, 1.0 / spectra), grid=(...  6.59 us
    unnamed x8, local copies, waits for them, and re-layouts  5.03 us
  transfers between devices with their start and end apart: 2, of which 2 were waited for; matrix products, arithmetic and copies ran while one was open for 0% of the time, Pallas kernels for 0%

profile of v1, /device:TPU:0, one launch (start us, length us, event | category | flops | bytes accessed | tf_op | source)
XLA Modules:
  0.0 139.4 jit_solution(4351049503179509498)
XLA Ops:
  6.5 0.0 all-gather.2.cloned.1.call-start
  6.5 0.0 copy-start.2
  6.5 1.0 copy-done.2
  7.6 0.0 copy-start.3
  7.6 0.8 copy-done.3
  8.3 17.3 %shard_map.37 = (bf16[832,256]{1,0:T(8,128)(2,1)S(1)}, f32[192,256]{1,0:T(8,128)S(1)}, f32[192,256]{1,0:T(8,128)S(1)}) custom-call(f32[4,2048]{1,0:T(4,128)S(1)} %copy-done.3, f32[64,2048]{1,0:T(8,128)S(1)} %copy-done.2, bf16[32768,256]{1,0:T(8,128)(2,1)} %frame_ref.1), custom_call_target="tpu_custom_call" | custom-call | tf_op jit(solution)/shard_map/pallas_call | solution.py:61
  25.6 1.3 collective-permute-start
  26.9 2.0 %collective-permute-done = f32[192,256]{1,0:T(8,128)S(1)} collective-permute-done((f32[192,256]{1,0:T(8,128)S(1)}, f32[192,256]{1,0:T(8,128)S(1)}, u32[]{:S(2)}, u32[]{:S(2)}) %collective-permute-start) | collective-permute-done | bytes 196640 | tf_op jit(solution)/shard_map/ppermute | solution.py:116
  29.0 0.2 reshape.6
  29.2 0.3 copy.10
  29.5 21.4 %all_to_all.5 = bf16[16,2,2,16,256]{4,3,2,1,0:T(8,128)(2,1)S(1)} all-to-all(bf16[16,2,2,16,256]{4,3,2,1,0:T(8,128)(2,1)S(1)} %bitcast.10), channel_id=1, replica_groups=mesh['chan'=16,'tile'=8] {'chan'}, dimensions={0} | all-to-all | bytes 1048576 | tf_op jit(solution)/shard_map/all_to_all | solution.py:120
  50.9 0.8 copy.8
  51.8 0.0 all-gather.2.cloned.1.call-update
  51.8 71.0 %all-gather.2.cloned.1.call-done.other_ref = bf16[8,2,512,256]{3,2,1,0:T(8,128)(2,1)} async-done(((bf16[1,2,512,256]{3,2,1,0:T(8,128)(2,1)}), bf16[8,2,512,256]{3,2,1,0:T(8,128)(2,1)}) %all-gather.2.cloned.1.call-update) | async-done | bytes 4194320 | tf_op jit(solution)/shard_map/all_gather | solution.py:122
  122.8 0.0 copy-start
  122.8 1.0 copy-done
  123.8 0.0 copy-start.1
  123.8 2.2 %copy-done.1 = bf16[8,2,512,256]{3,2,1,0:T(8,128)(2,1)S(1)} copy-done((bf16[8,2,512,256]{3,2,1,0:T(8,128)(2,1)S(1)}, bf16[8,2,512,256]{3,2,1,0:T(8,128)(2,1)}, u32[]{:S(2)}) %copy-start.1) | copy-done | bytes 4194328
  126.0 6.6 %shard_map.38 = f32[2,2,256,2048]{3,2,1,0:T(8,128)} custom-call(bf16[2,512,256]{2,1,0:T(8,128)(2,1)S(1)} %bitcast.9, bf16[8,2,512,256]{3,2,1,0:T(8,128)(2,1)S(1)} %copy-done.1), custom_call_target="tpu_custom_call" | custom-call | tf_op jit(solution)/shard_map/pallas_call | solution.py:97
  (2 shorter events, 0.1 us)
Async XLA Ops:
  6.5 116.2 %all-gather.2.cloned.1.call-start = ((), (), s32[]{:S(2)}) async-start(), calls=%async_computation.1 | async-start | bytes 4718592 | tf_op jit(solution)/shard_map/all_gather | solution.py:122
  6.5 1.0 copy-start.2
  7.6 0.8 copy-start.3
  25.6 3.3 %collective-permute-start = (f32[192,256]{1,0:T(8,128)S(1)}, f32[192,256]{1,0:T(8,128)S(1)}, u32[]{:S(2)}, u32[]{:S(2)}) collective-permute-start(f32[192,256]{1,0:T(8,128)S(1)} %get-tuple-element.10), channel_id=1, source_target_pairs={{8,0},{16,8},{24,16},{32,24},{40,32},{48,40},{56,48},{64,56},{72,6... | collective-permute-start | bytes 589832 | tf_op jit(solution)/shard_map/ppermute | solution.py:116
  122.8 1.0 copy-start
  123.8 2.2 %copy-start.1 = (bf16[8,2,512,256]{3,2,1,0:T(8,128)(2,1)S(1)}, bf16[8,2,512,256]{3,2,1,0:T(8,128)(2,1)}, u32[]{:S(2)}) copy-start(bf16[8,2,512,256]{3,2,1,0:T(8,128)(2,1)} %all-gather.2.cloned.1.call-done.other_ref) | copy-start | bytes 12582916
Sparse Core Ops, SparseCore 0:
  51.9 70.8 all-gather.1

commit v2 on v1

v2 whole, which is shorter than its diff:
```python
import functools
import math

import jax
import jax.numpy as jnp
import numpy as np
from jax import lax
from jax.experimental import pallas as pl
from jax.experimental.pallas import tpu as pltpu
from jax.sharding import PartitionSpec as P

MESH = pl.DeviceIdType.MESH
FFT = 2048
TAPS = 4
CHANNELS = 32
ROWS = 2 * CHANNELS
HALO = TAPS - 1
CHANS = 16
TILES = 8
RING = 4
FRAMES = 16
HALVES = 2
SPECTRA = FRAMES // HALVES
CH_DEV = CHANNELS // CHANS
INPUTS = 256
LANES = 128
PIECES = HALVES * CHANS
CUT = 9
CUT_A = 5
CUT_B = 12


def dft_rows():
    samples = np.arange(FFT, dtype=np.int64)
    centers = FFT // 8 + np.arange(CHANNELS, dtype=np.int64)
    angle = 2.0 * np.pi / FFT * (centers[:, None] * samples[None, :] % FFT)
    factor = 1.0 / math.sqrt(FFT)
    return np.concatenate([np.cos(angle), -np.sin(angle)], axis=0).astype(np.float32) * np.float32(factor)


def spread_kernel(
    taps_ref,
    table_ref,
    volt_ref,
    spread_ref,
    left_ref,
    frames,
    weights,
    sums,
    ahead,
    outbox,
    own,
    frame_sem,
    halo_send,
    halo_recv,
    turn_send,
    turn_recv,
    self_sem,
    ring_send,
    ring_recv,
    own_sem,
):
    chan = lax.axis_index("chan")
    tile = lax.axis_index("tile")
    row = tile // RING
    col = lax.rem(tile, RING)
    right = row * RING + lax.rem(col + 1, RING)
    left = row * RING + lax.rem(col + 3, RING)
    far = row * RING + lax.rem(col + 2, RING)
    other = (1 - row) * RING
    across = other + col
    across_right = other + lax.rem(col + 1, RING)
    across_left = other + lax.rem(col + 3, RING)
    across_far = other + lax.rem(col + 2, RING)

    def frame_copy(f):
        return pltpu.make_async_copy(volt_ref.at[pl.ds(f * FFT, FFT)], frames.at[f], frame_sem.at[f])

    @pl.loop(0, FRAMES)
    def _(f):
        frame_copy(f).start()

    barrier = pltpu.get_barrier_semaphore()

    @pl.loop(1, CHANS)
    def _(j):
        pl.semaphore_signal(barrier, inc=1, device_id=(lax.rem(chan + j, CHANS), tile), device_id_type=MESH)

    for peer in (right, left, across):
        pl.semaphore_signal(barrier, inc=1, device_id=(chan, peer), device_id_type=MESH)

    for t in range(TAPS):
        full = taps_ref[t : t + 1, :] * table_ref[...]
        high = full.astype(jnp.bfloat16)
        weights[2 * t * ROWS : (2 * t + 1) * ROWS, :] = high
        weights[(2 * t + 1) * ROWS : (2 * t + 2) * ROWS, :] = (full - high.astype(jnp.float32)).astype(jnp.bfloat16)
    sums[:, 0 : HALO * ROWS, :] = jnp.zeros((INPUTS // LANES, HALO * ROWS, LANES), jnp.float32)

    def channelize(start, stop):
        @pl.loop(start, stop)
        def _(f):
            frame_copy(f).wait()
            part = jnp.dot(weights[...], frames[f], preferred_element_type=jnp.float32)
            for t in range(TAPS):
                term = part[2 * t * ROWS : (2 * t + 1) * ROWS] + part[(2 * t + 1) * ROWS : (2 * t + 2) * ROWS]
                at = pl.ds(pl.multiple_of((f + HALO - t) * ROWS, ROWS), ROWS)
                for lane in range(INPUTS // LANES):
                    here = term[:, lane * LANES : (lane + 1) * LANES]
                    if t == 0:
                        sums[lane, at, :] = here
                    else:
                        sums[lane, at, :] += here

    def turn(h, j):
        peer = lax.rem(chan + j, CHANS)
        return pltpu.make_async_remote_copy(
            src_ref=outbox.at[h, peer],
            dst_ref=spread_ref.at[tile, h * CHANS + chan],
            send_sem=turn_send.at[h, peer],
            recv_sem=turn_recv.at[h, chan],
            device_id=(peer, tile),
            device_id_type=MESH,
        )

    def turned(h, j):
        peer = lax.rem(chan + j, CHANS)
        return pltpu.make_async_remote_copy(
            src_ref=outbox.at[h, peer],
            dst_ref=spread_ref.at[tile, h * CHANS + peer],
            send_sem=turn_send.at[h, peer],
            recv_sem=turn_recv.at[h, peer],
            device_id=(peer, tile),
            device_id_type=MESH,
        )

    def kept(h):
        return pltpu.make_async_copy(
            outbox.at[h, chan], spread_ref.at[tile, h * CHANS + chan], self_sem.at[h]
        )

    def send_turn(h):
        first = HALO + h * SPECTRA

        @pl.loop(0, CHANS)
        def _(p):
            for c in range(CH_DEV):
                base = first * ROWS + p * CH_DEV + c
                for lane in range(INPUTS // LANES):
                    real = sums[lane, pl.ds(base, SPECTRA, stride=ROWS), :]
                    imag = sums[lane, pl.ds(base + CHANNELS, SPECTRA, stride=ROWS), :]
                    both = jnp.concatenate([real, imag], axis=0).astype(jnp.bfloat16)
                    outbox[h, p, c, :, lane * LANES : (lane + 1) * LANES] = both

        @pl.loop(1, CHANS)
        def _(j):
            turn(h, j).start()

        kept(h).start()

    def wait_turn(h):
        @pl.loop(1, CHANS)
        def _(j):
            turned(h, j).wait_recv()

        kept(h).wait()

    def piece(h, start, stop):
        return pl.ds(h * CHANS + start, stop - start)

    part_a, part_b = (0, CUT), (CUT, CHANS)
    a_one, a_two = (0, CUT_A), (CUT_A, CUT)
    b_one, b_two = (CUT, CUT_B), (CUT_B, CHANS)
    kinds = (
        (right, tile, left, part_a),
        (right, tile, left, part_b),
        (right, across, across_left, part_a),
        (right, left, far, a_one),
        (right, left, far, b_one),
        (right, across_left, across_far, a_one),
        (left, tile, right, part_a),
        (left, tile, right, part_b),
        (left, across, across_right, part_a),
        (left, right, far, a_two),
        (left, right, far, b_two),
        (left, across_right, across_far, a_two),
        (across, tile, across, part_a),
        (across, tile, across, part_b),
        (across, left, across_left, part_b),
        (across, right, across_right, part_b),
        (across, far, across_far, b_one),
        (across, far, across_far, b_two),
    )

    def message(h, kind, arriving):
        to, sent, received, pieces = kinds[kind]
        slot = received if arriving else sent
        block = spread_ref.at[slot, piece(h, *pieces)]
        return pltpu.make_async_remote_copy(
            src_ref=block,
            dst_ref=block,
            send_sem=ring_send.at[h, kind],
            recv_sem=ring_recv.at[h, kind],
            device_id=(chan, to),
            device_id_type=MESH,
        )

    def send(h, *which):
        for kind in which:
            message(h, kind, False).start()

    def wait(h, *which):
        for kind in which:
            message(h, kind, True).wait_recv()

    def open_ring(h):
        wait_turn(h)
        send(h, 12, 0, 6, 1, 7, 13)

    def first_hops(h):
        wait(h, 12)
        send(h, 2, 8)
        wait(h, 1)
        send(h, 4, 14)
        wait(h, 7)
        send(h, 10, 15)

    def last_hops(h):
        wait(h, 0)
        send(h, 3)
        wait(h, 6)
        send(h, 9)
        wait(h, 4)
        send(h, 16)
        wait(h, 10)
        send(h, 17)
        wait(h, 2)
        send(h, 5)
        wait(h, 8)
        send(h, 11)

    channelize(0, HALO)
    pl.semaphore_wait(barrier, CHANS - 1 + 3)
    behind = pltpu.make_async_remote_copy(
        src_ref=sums.at[:, pl.ds(0, HALO * ROWS)],
        dst_ref=ahead,
        send_sem=halo_send,
        recv_sem=halo_recv,
        device_id=(lax.rem(chan + CHANS - 1, CHANS), tile),
        device_id_type=MESH,
    )
    behind.start()
    channelize(HALO, SPECTRA + HALO)
    send_turn(0)
    channelize(SPECTRA + HALO, FRAMES)
    behind.wait()
    ending = pl.ds(FRAMES * ROWS, HALO * ROWS)
    sums[:, ending, :] += jnp.where(chan == CHANS - 1, 0.0, ahead[...])
    send_turn(1)
    open_ring(0)
    first_hops(0)
    open_ring(1)
    fetch = pltpu.make_async_copy(spread_ref.at[tile], own, own_sem)
    fetch.start()
    last_hops(0)
    first_hops(1)
    last_hops(1)
    fetch.wait()
    for c in range(CH_DEV):
        mine = own[:, c].astype(jnp.float32).reshape(PIECES, 2, SPECTRA, INPUTS)
        swapped = jnp.stack([mine[:, 1], -mine[:, 0]], axis=1)
        depth = PIECES * 2 * SPECTRA
        left_ref[c, 0:INPUTS, :] = mine.reshape(depth, INPUTS).T.astype(jnp.bfloat16)
        left_ref[c, INPUTS : 2 * INPUTS, :] = swapped.reshape(depth, INPUTS).T.astype(jnp.bfloat16)
    for h in range(HALVES):
        wait(h, 3, 9, 5, 11, 13, 14, 15, 16, 17)
    for h in range(HALVES):
        for kind in range(len(kinds)):
            message(h, kind, False).wait_send()

        @pl.loop(1, CHANS)
        def _(j):
            turn(h, j).wait_send()


def spread(pfb_taps, voltages):
    kinds = 18
    depth = PIECES * 2 * SPECTRA
    vmem = pl.BlockSpec(memory_space=pltpu.VMEM)
    hbm = pl.BlockSpec(memory_space=pl.ANY)
    dma = pltpu.SemaphoreType.DMA
    return pl.pallas_call(
        spread_kernel,
        in_specs=[vmem, vmem, hbm],
        out_specs=[hbm, vmem],
        out_shape=[
            jax.ShapeDtypeStruct((TILES, PIECES, CH_DEV, 2 * SPECTRA, INPUTS), jnp.bfloat16),
            jax.ShapeDtypeStruct((CH_DEV, 2 * INPUTS, depth), jnp.bfloat16),
        ],
        scratch_shapes=[
            pltpu.VMEM((FRAMES, FFT, INPUTS), jnp.bfloat16),
            pltpu.VMEM((2 * TAPS * ROWS, FFT), jnp.bfloat16),
            pltpu.VMEM((INPUTS // LANES, (FRAMES + HALO) * ROWS, LANES), jnp.float32),
            pltpu.VMEM((INPUTS // LANES, HALO * ROWS, LANES), jnp.float32),
            pltpu.VMEM((HALVES, CHANS, CH_DEV, 2 * SPECTRA, INPUTS), jnp.bfloat16),
            pltpu.VMEM((PIECES, CH_DEV, 2 * SPECTRA, INPUTS), jnp.bfloat16),
            dma((FRAMES,)),
            dma,
            dma,
            dma((HALVES, CHANS)),
            dma((HALVES, CHANS)),
            dma((HALVES,)),
            dma((HALVES, kinds)),
            dma((HALVES, kinds)),
            dma,
        ],
        compiler_params=pltpu.CompilerParams(
            collective_id=0, has_side_effects=True, vmem_limit_bytes=48 << 20
        ),
    )(pfb_taps, dft_rows(), voltages)


def correlate_kernel(scale, left_ref, other_ref, out_ref):
    for q in range(other_ref.shape[0]):
        right = other_ref[q, :, 0].reshape(left_ref.shape[2], INPUTS)
        block = jnp.dot(left_ref[0], right, preferred_element_type=jnp.float32) * scale
        out_ref[0, 0, :, q * INPUTS : (q + 1) * INPUTS] = block[:INPUTS]
        out_ref[0, 1, :, q * INPUTS : (q + 1) * INPUTS] = block[INPUTS:]


def correlate(left, gathered):
    depth = left.shape[2]
    step = 2
    return pl.pallas_call(
        functools.partial(correlate_kernel, 1.0 / (CHANS * FRAMES)),
        grid=(CH_DEV, TILES // step),
        in_specs=[
            pl.BlockSpec((1, 2 * INPUTS, depth), lambda c, q: (c, 0, 0)),
            pl.BlockSpec((step, PIECES, 1, 2 * SPECTRA, INPUTS), lambda c, q: (q, 0, c, 0, 0)),
        ],
        out_specs=pl.BlockSpec((1, 2, INPUTS, step * INPUTS), lambda c, q: (c, 0, 0, q)),
        out_shape=jax.ShapeDtypeStruct((CH_DEV, 2, INPUTS, TILES * INPUTS), jnp.float32),
        compiler_params=pltpu.CompilerParams(vmem_limit_bytes=32 << 20),
    )(left, gathered)


def shards(voltages, pfb_taps):
    gathered, left = spread(pfb_taps, voltages)
    return correlate(left, gathered)


def solution(mesh):
    placed = (P("chan", "tile"), P())
    return jax.shard_map(
        shards, mesh=mesh, in_specs=placed, out_specs=P("chan", None, "tile", None), check_vma=False
    )
```

time: 140 us -> 61.3 us (0.44)
  waiting for transfers between devices: 73 us -> 0 us
  Pallas kernels: 23.9 us -> 59.3 us
  blocking collectives: 21.4 us -> 0 us
  between operations: 13.4 us -> 0.01 us
  local copies, waits for them, and re-layouts: 6.35 us -> 1.8 us
    all_gather x1 -> x0, waiting for transfers between devices: 71 us -> none  [shards(): gathered = lax.all_gather(own, 'tile', axis=0, tiled=False)]
    pallas_call x2, Pallas kernels: 23.9 us -> 59.3 us  [the longest x1 53 us: spread(): pl.pallas_call(spread_kernel, in_specs=[vmem, vmem, hbm], out_specs=[hbm,...]
    all_to_all x1 -> x0, blocking collectives: 21.4 us -> none  [shards(): lax.all_to_all(spectra, 'chan', split_axis=0, concat_axis=0, tiled=True)]
    unnamed x8 -> x4, local copies, waits for them, and re-layouts: 5.03 us -> 1.8 us
    ppermute x1 -> x0, waiting for transfers between devices: 2.04 us -> none  [shards(): arrived = lax.ppermute(head, 'chan', [(i + 1, i) for i in range(chans - 1)])]
  transfers between devices with their start and end apart: 2 -> 0, of which waited for: 2 -> 0; matrix products, arithmetic and copies ran while one was open for 0% -> 0% of each run, Pallas kernels for 0% -> 0%
where the time goes in v2:
time: 61.3 us; the launch traced here: 61.1 us
  Pallas kernels  59.3 us (97%)
  local copies, waits for them, and re-layouts  1.8 us (3%)
    pallas_call x1, Pallas kernels, spread(): pl.pallas_call(spread_kernel, in_specs=[vmem, vmem, hbm], out_specs=[hbm,...  53 us
    pallas_call x1, Pallas kernels, correlate(): pl.pallas_call(functools.partial(correlate_kernel, 1.0 / (CHANS * FRAMES)...  6.31 us
    unnamed x4, local copies, waits for them, and re-layouts  1.8 us

profile of v2, /device:TPU:0, one launch (start us, length us, event | category | flops | bytes accessed | tf_op | source)
XLA Modules:
  0.0 61.1 jit_solution(7464351980223542769)
XLA Ops:
  0.0 0.0 copy-start
  0.0 1.0 %copy-done = f32[64,2048]{1,0:T(8,128)S(1)} copy-done((f32[64,2048]{1,0:T(8,128)S(1)}, f32[64,2048]{1,0:T(8,128)}, u32[]{:S(2)}) %copy-start) | copy-done | bytes 524312
  1.0 0.0 copy-start.1
  1.0 0.8 %copy-done.1 = f32[4,2048]{1,0:T(4,128)S(1)} copy-done((f32[4,2048]{1,0:T(4,128)S(1)}, f32[4,2048]{1,0:T(4,128)}, u32[]{:S(2)}) %copy-start.1) | copy-done | bytes 32792
  1.8 53.0 %shard_map.37 = (bf16[8,32,2,16,256]{4,3,2,1,0:T(8,128)(2,1)S(1)}, bf16[2,512,512]{2,1,0:T(8,128)(2,1)S(1)}) custom-call(f32[4,2048]{1,0:T(4,128)S(1)} %copy-done.1, f32[64,2048]{1,0:T(8,128)S(1)} %copy-done, bf16[32768,256]{1,0:T(8,128)(2,1)} %volt_ref.1), custom_call_target="tpu_custom_call" | custom-call | tf_op jit(solution)/shard_map/pallas_call | solution.py:291
  54.8 6.3 %shard_map.38 = f32[2,2,256,2048]{3,2,1,0:T(8,128)} custom-call(bf16[2,512,512]{2,1,0:T(8,128)(2,1)S(1)} %get-tuple-element.7.left_ref, bf16[8,32,2,16,256]{4,3,2,1,0:T(8,128)(2,1)S(1)} %get-tuple-element.8.other_ref), custom_call_target="tpu_custom_call" | custom-call | tf_op jit(solution)/shard_map/pallas_call | solution.py:333
Async XLA Ops:
  0.0 1.0 %copy-start = (f32[64,2048]{1,0:T(8,128)S(1)}, f32[64,2048]{1,0:T(8,128)}, u32[]{:S(2)}) copy-start(f32[64,2048]{1,0:T(8,128)} %constant.2.clone.table_ref) | copy-start | bytes 1572868
  1.0 0.8 %copy-start.1 = (f32[4,2048]{1,0:T(4,128)S(1)}, f32[4,2048]{1,0:T(4,128)}, u32[]{:S(2)}) copy-start(f32[4,2048]{1,0:T(4,128)} %taps_ref.1) | copy-start | bytes 98308

commit v3 on v2

v3 whole, which is shorter than its diff:
```python
import functools
import math

import jax
import jax.numpy as jnp
import numpy as np
from jax import lax
from jax.experimental import pallas as pl
from jax.experimental.pallas import tpu as pltpu
from jax.sharding import PartitionSpec as P

MESH = pl.DeviceIdType.MESH
FFT = 2048
TAPS = 4
CHANNELS = 32
ROWS = 2 * CHANNELS
HALO = TAPS - 1
CHANS = 16
TILES = 8
RING = 4
FRAMES = 16
PARTS = 4
SPECTRA = FRAMES // PARTS
BLOCK = 2 * SPECTRA
CHUNKS = ((0, 2), (2, 4))
PAUSE = 16
STEP = 2
CH_DEV = CHANNELS // CHANS
INPUTS = 256
LANES = 128
DEPTH = 2 * FRAMES * CHANS
CUT = 9
CUT_A = 5
CUT_B = 12


def dft_rows():
    samples = np.arange(FFT, dtype=np.int64)
    centers = FFT // 8 + np.arange(CHANNELS, dtype=np.int64)
    angle = 2.0 * np.pi / FFT * (centers[:, None] * samples[None, :] % FFT)
    factor = 1.0 / math.sqrt(FFT)
    return np.concatenate([np.cos(angle), -np.sin(angle)], axis=0).astype(np.float32) * np.float32(factor)


def folded(pfb_taps):
    full = pfb_taps[:, None, :] * dft_rows()[None]
    high = lax.reduce_precision(full, 8, 7)
    shape = (TAPS * ROWS, FFT)
    return high.astype(jnp.bfloat16).reshape(shape), (full - high).astype(jnp.bfloat16).reshape(shape)


def spread_kernel(
    high_ref,
    low_ref,
    volt_ref,
    spread_ref,
    left_ref,
    frames,
    weights,
    sums,
    ahead,
    outbox,
    own,
    frame_sem,
    halo_send,
    halo_recv,
    turn_send,
    turn_recv,
    self_sem,
    ring_send,
    ring_recv,
    own_sem,
):
    chan = lax.axis_index("chan")
    tile = lax.axis_index("tile")
    row = tile // RING
    col = lax.rem(tile, RING)
    right = row * RING + lax.rem(col + 1, RING)
    left = row * RING + lax.rem(col + 3, RING)
    far = row * RING + lax.rem(col + 2, RING)
    other = (1 - row) * RING
    across = other + col
    across_right = other + lax.rem(col + 1, RING)
    across_left = other + lax.rem(col + 3, RING)
    across_far = other + lax.rem(col + 2, RING)

    def frame_copy(f):
        return pltpu.make_async_copy(volt_ref.at[pl.ds(f * FFT, FFT)], frames.at[f], frame_sem.at[f])

    @pl.loop(0, FRAMES)
    def _(f):
        frame_copy(f).start()

    barrier = pltpu.get_barrier_semaphore()

    @pl.loop(1, CHANS)
    def _(j):
        pl.semaphore_signal(barrier, inc=1, device_id=(lax.rem(chan + j, CHANS), tile), device_id_type=MESH)

    for peer in (right, left, across):
        pl.semaphore_signal(barrier, inc=1, device_id=(chan, peer), device_id_type=MESH)

    weights[0 : TAPS * ROWS, :] = high_ref[...]
    weights[TAPS * ROWS :, :] = low_ref[...]
    sums[:, 0 : HALO * ROWS, :] = jnp.zeros((INPUTS // LANES, HALO * ROWS, LANES), jnp.float32)

    def channelize(start, stop):
        @pl.loop(start, stop)
        def _(f):
            frame_copy(f).wait()
            part = jnp.dot(weights[...], frames[f], preferred_element_type=jnp.float32)
            for t in range(TAPS):
                term = part[t * ROWS : (t + 1) * ROWS] + part[(TAPS + t) * ROWS : (TAPS + t + 1) * ROWS]
                at = pl.ds(pl.multiple_of((f + HALO - t) * ROWS, ROWS), ROWS)
                for lane in range(INPUTS // LANES):
                    here = term[:, lane * LANES : (lane + 1) * LANES]
                    if t == 0:
                        sums[lane, at, :] = here
                    else:
                        sums[lane, at, :] += here

    def rows(h):
        first, last = CHUNKS[h]
        return pl.ds(first * BLOCK, (last - first) * BLOCK)

    def turn(h, j, arriving):
        peer = lax.rem(chan + j, CHANS)
        return pltpu.make_async_remote_copy(
            src_ref=outbox.at[peer, :, rows(h)],
            dst_ref=spread_ref.at[tile, peer if arriving else chan, :, rows(h)],
            send_sem=turn_send.at[h, peer],
            recv_sem=turn_recv.at[h, peer if arriving else chan],
            device_id=(peer, tile),
            device_id_type=MESH,
        )

    def kept(h):
        return pltpu.make_async_copy(
            outbox.at[chan, :, rows(h)], spread_ref.at[tile, chan, :, rows(h)], self_sem.at[h]
        )

    def send_turn(h):
        @pl.loop(0, CHANS)
        def _(p):
            for c in range(CH_DEV):
                for part in range(*CHUNKS[h]):
                    base = (HALO + part * SPECTRA) * ROWS + p * CH_DEV + c
                    for lane in range(INPUTS // LANES):
                        real = sums[lane, pl.ds(base, SPECTRA, stride=ROWS), :]
                        imag = sums[lane, pl.ds(base + CHANNELS, SPECTRA, stride=ROWS), :]
                        both = jnp.concatenate([real, imag], axis=0).astype(jnp.bfloat16)
                        outbox[p, c, part * BLOCK : (part + 1) * BLOCK, lane * LANES : (lane + 1) * LANES] = both

        @pl.loop(1, CHANS)
        def _(j):
            turn(h, j, False).start()

        kept(h).start()

    def wait_turn(h):
        @pl.loop(1, CHANS)
        def _(j):
            turn(h, j, True).wait_recv()

        kept(h).wait()

    part_a, part_b = (0, CUT), (CUT, CHANS)
    a_one, a_two = (0, CUT_A), (CUT_A, CUT)
    b_one, b_two = (CUT, CUT_B), (CUT_B, CHANS)
    kinds = (
        (right, tile, left, part_a),
        (right, tile, left, part_b),
        (right, across, across_left, part_a),
        (right, left, far, a_one),
        (right, left, far, b_one),
        (right, across_left, across_far, a_one),
        (left, tile, right, part_a),
        (left, tile, right, part_b),
        (left, across, across_right, part_a),
        (left, right, far, a_two),
        (left, right, far, b_two),
        (left, across_right, across_far, a_two),
        (across, tile, across, part_a),
        (across, tile, across, part_b),
        (across, left, across_left, part_b),
        (across, right, across_right, part_b),
        (across, far, across_far, b_one),
        (across, far, across_far, b_two),
    )

    def message(h, kind, arriving):
        to, sent, received, pieces = kinds[kind]
        slot = received if arriving else sent
        block = spread_ref.at[slot, pl.ds(pieces[0], pieces[1] - pieces[0]), :, rows(h)]
        return pltpu.make_async_remote_copy(
            src_ref=block,
            dst_ref=block,
            send_sem=ring_send.at[h, kind],
            recv_sem=ring_recv.at[h, kind],
            device_id=(chan, to),
            device_id_type=MESH,
        )

    def send(h, *which):
        for kind in which:
            message(h, kind, False).start()

    def wait(h, *which):
        for kind in which:
            message(h, kind, True).wait_recv()

    def open_ring(h):
        wait_turn(h)
        send(h, 12, 0, 6, 1, 7, 13)

    def first_hops(h):
        wait(h, 12)
        send(h, 2, 8)
        wait(h, 1)
        send(h, 4, 14)
        wait(h, 7)
        send(h, 10, 15)

    def last_hops(h):
        wait(h, 0)
        send(h, 3)
        wait(h, 6)
        send(h, 9)
        wait(h, 4)
        send(h, 16)
        wait(h, 10)
        send(h, 17)
        wait(h, 2)
        send(h, 5)
        wait(h, 8)
        send(h, 11)

    channelize(0, HALO)
    pl.semaphore_wait(barrier, CHANS - 1 + 3)
    behind = pltpu.make_async_remote_copy(
        src_ref=sums.at[:, pl.ds(0, HALO * ROWS)],
        dst_ref=ahead,
        send_sem=halo_send,
        recv_sem=halo_recv,
        device_id=(lax.rem(chan + CHANS - 1, CHANS), tile),
        device_id_type=MESH,
    )
    behind.start()
    ready = [last * SPECTRA + HALO for _, last in CHUNKS[:-1]]
    channelize(HALO, ready[0])
    send_turn(0)
    channelize(ready[0], PAUSE)
    open_ring(0)
    channelize(PAUSE, FRAMES)
    behind.wait()
    ending = pl.ds(FRAMES * ROWS, HALO * ROWS)
    sums[:, ending, :] += jnp.where(chan == CHANS - 1, 0.0, ahead[...])
    send_turn(1)
    first_hops(0)
    open_ring(1)
    fetch = pltpu.make_async_copy(spread_ref.at[tile], own, own_sem)
    fetch.start()
    last_hops(0)
    fetch.wait()

    def prepare(c):
        mine = own[:, c].astype(jnp.float32).reshape(DEPTH, INPUTS).T
        at = lax.broadcasted_iota(jnp.int32, mine.shape, 1)
        upper = lax.rem(at, BLOCK) < SPECTRA
        swapped = jnp.where(upper, jnp.roll(mine, -SPECTRA, axis=1), -jnp.roll(mine, SPECTRA, axis=1))
        left_ref[c, 0:INPUTS, :] = mine.astype(jnp.bfloat16)
        left_ref[c, INPUTS : 2 * INPUTS, :] = swapped.astype(jnp.bfloat16)

    prepare(0)
    first_hops(1)
    prepare(1)
    last_hops(1)
    for h in range(len(CHUNKS)):
        wait(h, 3, 9, 5, 11, 13, 14, 15, 16, 17)
    for h in range(len(CHUNKS)):
        for kind in range(len(kinds)):
            message(h, kind, False).wait_send()

        @pl.loop(1, CHANS)
        def _(j):
            turn(h, j, False).wait_send()


def spread(high, low, voltages):
    kinds = 18
    chunks = len(CHUNKS)
    vmem = pl.BlockSpec(memory_space=pltpu.VMEM)
    hbm = pl.BlockSpec(memory_space=pltpu.HBM)
    dma = pltpu.SemaphoreType.DMA
    return pl.pallas_call(
        spread_kernel,
        in_specs=[vmem, vmem, hbm],
        out_specs=[vmem, vmem],
        out_shape=[
            jax.ShapeDtypeStruct((TILES, CHANS, CH_DEV, 2 * FRAMES, INPUTS), jnp.bfloat16),
            jax.ShapeDtypeStruct((CH_DEV, 2 * INPUTS, DEPTH), jnp.bfloat16),
        ],
        scratch_shapes=[
            pltpu.VMEM((FRAMES, FFT, INPUTS), jnp.bfloat16),
            pltpu.VMEM((2 * TAPS * ROWS, FFT), jnp.bfloat16),
            pltpu.VMEM((INPUTS // LANES, (FRAMES + HALO) * ROWS, LANES), jnp.float32),
            pltpu.VMEM((INPUTS // LANES, HALO * ROWS, LANES), jnp.float32),
            pltpu.VMEM((CHANS, CH_DEV, 2 * FRAMES, INPUTS), jnp.bfloat16),
            pltpu.VMEM((CHANS, CH_DEV, 2 * FRAMES, INPUTS), jnp.bfloat16),
            dma((FRAMES,)),
            dma,
            dma,
            dma((chunks, CHANS)),
            dma((chunks, CHANS)),
            dma((chunks,)),
            dma((chunks, kinds)),
            dma((chunks, kinds)),
            dma,
        ],
        compiler_params=pltpu.CompilerParams(
            collective_id=0, has_side_effects=True, vmem_limit_bytes=44 << 20
        ),
    )(high, low, voltages)


def correlate_kernel(scale, left_ref, other_ref, out_ref, planes, sems):
    copies = []
    for c in range(CH_DEV):
        for q in range(TILES):
            right = other_ref[q, :, c].reshape(DEPTH, INPUTS)
            block = jnp.dot(left_ref[c], right, preferred_element_type=jnp.float32) * scale
            planes[c, 0, :, q * INPUTS : (q + 1) * INPUTS] = block[:INPUTS]
            planes[c, 1, :, q * INPUTS : (q + 1) * INPUTS] = block[INPUTS:]
            if (q + 1) % STEP == 0:
                columns = pl.ds((q + 1 - STEP) * INPUTS, STEP * INPUTS)
                copies.append(
                    pltpu.make_async_copy(
                        planes.at[c, :, :, columns], out_ref.at[c, :, :, columns], sems.at[len(copies)]
                    )
                )
                copies[-1].start()
    for copy in copies:
        copy.wait()


def correlate(left, gathered):
    vmem = pl.BlockSpec(memory_space=pltpu.VMEM)
    shape = (CH_DEV, 2, INPUTS, TILES * INPUTS)
    return pl.pallas_call(
        functools.partial(correlate_kernel, 1.0 / (CHANS * FRAMES)),
        in_specs=[vmem, vmem],
        out_specs=pl.BlockSpec(memory_space=pltpu.HBM),
        out_shape=jax.ShapeDtypeStruct(shape, jnp.float32),
        scratch_shapes=[
            pltpu.VMEM(shape, jnp.float32),
            pltpu.SemaphoreType.DMA((CH_DEV * TILES // STEP,)),
        ],
        compiler_params=pltpu.CompilerParams(vmem_limit_bytes=16 << 20),
    )(left, gathered)


def shards(voltages, pfb_taps):
    gathered, left = spread(*folded(pfb_taps), voltages)
    return correlate(left, gathered)


def solution(mesh):
    placed = (P("chan", "tile"), P())
    return jax.shard_map(
        shards, mesh=mesh, in_specs=placed, out_specs=P("chan", None, "tile", None), check_vma=False
    )
```

time: 61.3 us -> 57.9 us (0.945)
  Pallas kernels: 59.3 us -> 56.1 us
  local copies, waits for them, and re-layouts: 1.8 us -> 0 us
  other arithmetic: 0 us -> 1.59 us
    pallas_call x1, Pallas kernels: 6.31 us -> 3.81 us  [correlate(): pl.pallas_call(functools.partial(correlate_kernel, 1.0 / (CHANS * FRAMES)...]
    unnamed x4 -> x0, local copies, waits for them, and re-layouts: 1.8 us -> none
    mul x0 -> x1, other arithmetic: none -> 1.27 us  [folded(): full = pfb_taps[:, None, :] * dft_rows()[None]]
    pallas_call x1, Pallas kernels: 53 us -> 52.3 us  [spread(): pl.pallas_call(spread_kernel, in_specs=[vmem, vmem, hbm], out_specs=[vmem...]
where the time goes in v3:
time: 57.9 us; the launch traced here: 57.7 us
  Pallas kernels  56.1 us (97%)
  other arithmetic  1.59 us (3%)
    pallas_call x1, Pallas kernels, spread(): pl.pallas_call(spread_kernel, in_specs=[vmem, vmem, hbm], out_specs=[vmem...  52.3 us
    pallas_call x1, Pallas kernels, correlate(): pl.pallas_call(functools.partial(correlate_kernel, 1.0 / (CHANS * FRAMES)...  3.81 us
    mul x1, other arithmetic, folded(): full = pfb_taps[:, None, :] * dft_rows()[None]  1.27 us

profile of v3, /device:TPU:0, one launch (start us, length us, event | category | flops | bytes accessed | tf_op | source)
XLA Modules:
  0.0 57.7 jit_solution(6764384389526842131)
XLA Ops:
  0.0 1.3 %broadcast_multiply_fusion = f32[4,64,2048]{2,1,0:T(8,128)S(1)} fusion(f32[64,2048]{1,0:T(8,128)} %constant.3, f32[4,2048]{1,0:T(4,128)} %param.4), kind=kLoop, calls=%fused_computation.3 | loop fusion | flops 524288 | bytes 2654208 | tf_op jit(solution)/shard_map/mul | solution.py:46
  1.3 0.3 fusion
  1.6 52.3 %shard_map.37 = (bf16[8,16,2,32,256]{4,3,2,1,0:T(8,128)(2,1)S(1)}, bf16[2,512,512]{2,1,0:T(8,128)(2,1)S(1)}) custom-call(bf16[256,2048]{1,0:T(8,128)(2,1)S(1)} %get-tuple-element.10.high_ref, bf16[256,2048]{1,0:T(8,128)(2,1)S(1)} %get-tuple-element.9.low_ref, bf16[32768,256]{1,0:T(8,128)(2,1)} %volt_ref.1), custom_call_target="tpu_custom_call" | custom-call | tf_op jit(solution)/shard_map/pallas_call | solution.py:295
  53.9 3.8 %shard_map.38 = f32[2,2,256,2048]{3,2,1,0:T(8,128)} custom-call(bf16[2,512,512]{2,1,0:T(8,128)(2,1)S(1)} %get-tuple-element.7.left_ref, bf16[8,16,2,32,256]{4,3,2,1,0:T(8,128)(2,1)S(1)} %get-tuple-element.8.other_ref), custom_call_target="tpu_custom_call" | custom-call | tf_op jit(solution)/shard_map/pallas_call | solution.py:349

commit v4 on v3

--- a/solution.py
+++ b/solution.py
@@ -19,10 +19,10 @@
 TILES = 8
 RING = 4
 FRAMES = 16
-PARTS = 4
+PARTS = 2
 SPECTRA = FRAMES // PARTS
 BLOCK = 2 * SPECTRA
-CHUNKS = ((0, 2), (2, 4))
+CHUNKS = ((0, 1), (1, 2))
 PAUSE = 16
 STEP = 2
 CH_DEV = CHANNELS // CHANS
@@ -104,30 +104,37 @@
     weights[TAPS * ROWS :, :] = low_ref[...]
     sums[:, 0 : HALO * ROWS, :] = jnp.zeros((INPUTS // LANES, HALO * ROWS, LANES), jnp.float32)
 
+    def add_frame(part, f):
+        for t in range(TAPS):
+            term = part[t * ROWS : (t + 1) * ROWS] + part[(TAPS + t) * ROWS : (TAPS + t + 1) * ROWS]
+            at = pl.ds(pl.multiple_of((f + HALO - t) * ROWS, ROWS), ROWS)
+            for lane in range(INPUTS // LANES):
+                here = term[:, lane * LANES : (lane + 1) * LANES]
+                if t == 0:
+                    sums[lane, at, :] = here
+                else:
+                    sums[lane, at, :] += here
+
     def channelize(start, stop):
-        @pl.loop(start, stop)
-        def _(f):
+        @pl.loop(0, (stop - start) // 2)
+        def _(g):
+            f = start + 2 * g
             frame_copy(f).wait()
-            part = jnp.dot(weights[...], frames[f], preferred_element_type=jnp.float32)
-            for t in range(TAPS):
-                term = part[t * ROWS : (t + 1) * ROWS] + part[(TAPS + t) * ROWS : (TAPS + t + 1) * ROWS]
-                at = pl.ds(pl.multiple_of((f + HALO - t) * ROWS, ROWS), ROWS)
-                for lane in range(INPUTS // LANES):
-                    here = term[:, lane * LANES : (lane + 1) * LANES]
-                    if t == 0:
-                        sums[lane, at, :] = here
-                    else:
-                        sums[lane, at, :] += here
-
-    def rows(h):
-        first, last = CHUNKS[h]
-        return pl.ds(first * BLOCK, (last - first) * BLOCK)
+            frame_copy(f + 1).wait()
+            pair = jnp.concatenate([frames[f], frames[f + 1]], axis=1)
+            part = jnp.dot(weights[...], pair, preferred_element_type=jnp.float32)
+            add_frame(part[:, :INPUTS], f)
+            add_frame(part[:, INPUTS:], f + 1)
+
+        if (stop - start) % 2:
+            frame_copy(stop - 1).wait()
+            add_frame(jnp.dot(weights[...], frames[stop - 1], preferred_element_type=jnp.float32), stop - 1)
 
     def turn(h, j, arriving):
         peer = lax.rem(chan + j, CHANS)
         return pltpu.make_async_remote_copy(
-            src_ref=outbox.at[peer, :, rows(h)],
-            dst_ref=spread_ref.at[tile, peer if arriving else chan, :, rows(h)],
+            src_ref=outbox.at[h, peer],
+            dst_ref=spread_ref.at[tile, h * CHANS + (peer if arriving else chan)],
             send_sem=turn_send.at[h, peer],
             recv_sem=turn_recv.at[h, peer if arriving else chan],
             device_id=(peer, tile),
@@ -136,7 +143,7 @@
 
     def kept(h):
         return pltpu.make_async_copy(
-            outbox.at[chan, :, rows(h)], spread_ref.at[tile, chan, :, rows(h)], self_sem.at[h]
+            outbox.at[h, chan], spread_ref.at[tile, h * CHANS + chan], self_sem.at[h]
         )
 
     def send_turn(h):
@@ -149,7 +156,7 @@
                         real = sums[lane, pl.ds(base, SPECTRA, stride=ROWS), :]
                         imag = sums[lane, pl.ds(base + CHANNELS, SPECTRA, stride=ROWS), :]
                         both = jnp.concatenate([real, imag], axis=0).astype(jnp.bfloat16)
-                        outbox[p, c, part * BLOCK : (part + 1) * BLOCK, lane * LANES : (lane + 1) * LANES] = both
+                        outbox[part, p, c, :, lane * LANES : (lane + 1) * LANES] = both
 
         @pl.loop(1, CHANS)
         def _(j):
@@ -191,7 +198,7 @@
     def message(h, kind, arriving):
         to, sent, received, pieces = kinds[kind]
         slot = received if arriving else sent
-        block = spread_ref.at[slot, pl.ds(pieces[0], pieces[1] - pieces[0]), :, rows(h)]
+        block = spread_ref.at[slot, pl.ds(h * CHANS + pieces[0], pieces[1] - pieces[0])]
         return pltpu.make_async_remote_copy(
             src_ref=block,
             dst_ref=block,
@@ -211,7 +218,7 @@
 
     def open_ring(h):
         wait_turn(h)
-        send(h, 12, 0, 6, 1, 7, 13)
+        send(h, 12, 1, 7, 0, 6, 13)
 
     def first_hops(h):
         wait(h, 12)
@@ -235,7 +242,7 @@
         wait(h, 8)
         send(h, 11)
 
-    channelize(0, HALO)
+    channelize(0, HALO + 1)
     pl.semaphore_wait(barrier, CHANS - 1 + 3)
     behind = pltpu.make_async_remote_copy(
         src_ref=sums.at[:, pl.ds(0, HALO * ROWS)],
@@ -247,7 +254,7 @@
     )
     behind.start()
     ready = [last * SPECTRA + HALO for _, last in CHUNKS[:-1]]
-    channelize(HALO, ready[0])
+    channelize(HALO + 1, ready[0])
     send_turn(0)
     channelize(ready[0], PAUSE)
     open_ring(0)
@@ -297,7 +304,7 @@
         in_specs=[vmem, vmem, hbm],
         out_specs=[vmem, vmem],
         out_shape=[
-            jax.ShapeDtypeStruct((TILES, CHANS, CH_DEV, 2 * FRAMES, INPUTS), jnp.bfloat16),
+            jax.ShapeDtypeStruct((TILES, PARTS * CHANS, CH_DEV, BLOCK, INPUTS), jnp.bfloat16),
             jax.ShapeDtypeStruct((CH_DEV, 2 * INPUTS, DEPTH), jnp.bfloat16),
         ],
         scratch_shapes=[
@@ -305,8 +312,8 @@
             pltpu.VMEM((2 * TAPS * ROWS, FFT), jnp.bfloat16),
             pltpu.VMEM((INPUTS // LANES, (FRAMES + HALO) * ROWS, LANES), jnp.float32),
             pltpu.VMEM((INPUTS // LANES, HALO * ROWS, LANES), jnp.float32),
-            pltpu.VMEM((CHANS, CH_DEV, 2 * FRAMES, INPUTS), jnp.bfloat16),
-            pltpu.VMEM((CHANS, CH_DEV, 2 * FRAMES, INPUTS), jnp.bfloat16),
+            pltpu.VMEM((PARTS, CHANS, CH_DEV, BLOCK, INPUTS), jnp.bfloat16),
+            pltpu.VMEM((PARTS * CHANS, CH_DEV, BLOCK, INPUTS), jnp.bfloat16),
             dma((FRAMES,)),
             dma,
             dma,

time: 57.9 us -> 57.2 us (0.988)
  Pallas kernels: 56.1 us -> 55.4 us
    pallas_call x1, Pallas kernels: 52.3 us -> 51.6 us  [spread(): pl.pallas_call(spread_kernel, in_specs=[vmem, vmem, hbm], out_specs=[vmem...]
where the time goes in v4:
time: 57.2 us; the launch traced here: 57 us
  Pallas kernels  55.4 us (97%)
  other arithmetic  1.59 us (3%)
    pallas_call x1, Pallas kernels, spread(): pl.pallas_call(spread_kernel, in_specs=[vmem, vmem, hbm], out_specs=[vmem...  51.6 us
    pallas_call x1, Pallas kernels, correlate(): pl.pallas_call(functools.partial(correlate_kernel, 1.0 / (CHANS * FRAMES)...  3.82 us
    mul x1, other arithmetic, folded(): full = pfb_taps[:, None, :] * dft_rows()[None]  1.27 us

profile of v4, /device:TPU:0, one launch (start us, length us, event | category | flops | bytes accessed | tf_op | source)
XLA Modules:
  0.0 57.0 jit_solution(17469007051504544464)
XLA Ops:
  0.0 1.3 %broadcast_multiply_fusion = f32[4,64,2048]{2,1,0:T(8,128)S(1)} fusion(f32[64,2048]{1,0:T(8,128)} %constant.3, f32[4,2048]{1,0:T(4,128)} %param.4), kind=kLoop, calls=%fused_computation.3 | loop fusion | flops 524288 | bytes 2654208 | tf_op jit(solution)/shard_map/mul | solution.py:46
  1.3 0.3 fusion
  1.6 51.6 %shard_map.37 = (bf16[8,32,2,16,256]{4,3,2,1,0:T(8,128)(2,1)S(1)}, bf16[2,512,512]{2,1,0:T(8,128)(2,1)S(1)}) custom-call(bf16[256,2048]{1,0:T(8,128)(2,1)S(1)} %get-tuple-element.10.high_ref, bf16[256,2048]{1,0:T(8,128)(2,1)S(1)} %get-tuple-element.9.low_ref, bf16[32768,256]{1,0:T(8,128)(2,1)} %volt_ref.1), custom_call_target="tpu_custom_call" | custom-call | tf_op jit(solution)/shard_map/pallas_call | solution.py:302
  53.2 3.8 %shard_map.38 = f32[2,2,256,2048]{3,2,1,0:T(8,128)} custom-call(bf16[2,512,512]{2,1,0:T(8,128)(2,1)S(1)} %get-tuple-element.7.left_ref, bf16[8,32,2,16,256]{4,3,2,1,0:T(8,128)(2,1)S(1)} %get-tuple-element.8.other_ref), custom_call_target="tpu_custom_call" | custom-call | tf_op jit(solution)/shard_map/pallas_call | solution.py:356

commit v5 on v4

--- a/solution.py
+++ b/solution.py
@@ -45,8 +45,7 @@
 def folded(pfb_taps):
     full = pfb_taps[:, None, :] * dft_rows()[None]
     high = lax.reduce_precision(full, 8, 7)
-    shape = (TAPS * ROWS, FFT)
-    return high.astype(jnp.bfloat16).reshape(shape), (full - high).astype(jnp.bfloat16).reshape(shape)
+    return high.astype(jnp.bfloat16), (full - high).astype(jnp.bfloat16)
 
 
 def spread_kernel(
@@ -100,8 +99,9 @@
     for peer in (right, left, across):
         pl.semaphore_signal(barrier, inc=1, device_id=(chan, peer), device_id_type=MESH)
 
-    weights[0 : TAPS * ROWS, :] = high_ref[...]
-    weights[TAPS * ROWS :, :] = low_ref[...]
+    for t in range(TAPS):
+        weights[t * ROWS : (t + 1) * ROWS, :] = high_ref[t]
+        weights[(TAPS + t) * ROWS : (TAPS + t + 1) * ROWS, :] = low_ref[t]
     sums[:, 0 : HALO * ROWS, :] = jnp.zeros((INPUTS // LANES, HALO * ROWS, LANES), jnp.float32)
 
     def add_frame(part, f):

time: 57.2 us -> 57 us (level)
    mul x1 -> x0, other arithmetic: 1.27 us -> none  [folded(): full = pfb_taps[:, None, :] * dft_rows()[None]]
    convert_element_type x1, other arithmetic: 0.32 us -> 1.42 us  [folded(): return (high.astype(jnp.bfloat16), (full - high).astype(jnp.bfloat16))]
where the time goes in v5:
time: 57 us; the launch traced here: 56.9 us
  Pallas kernels  55.4 us (97%)
  other arithmetic  1.42 us (2%)
    pallas_call x1, Pallas kernels, spread(): pl.pallas_call(spread_kernel, in_specs=[vmem, vmem, hbm], out_specs=[vmem...  51.6 us
    pallas_call x1, Pallas kernels, correlate(): pl.pallas_call(functools.partial(correlate_kernel, 1.0 / (CHANS * FRAMES)...  3.82 us
    convert_element_type x1, other arithmetic, folded(): return (high.astype(jnp.bfloat16), (full - high).astype(jnp.bfloat16))  1.42 us

profile of v5, /device:TPU:0, one launch (start us, length us, event | category | flops | bytes accessed | tf_op | source)
XLA Modules:
  0.0 56.9 jit_solution(12712200500026895138)
XLA Ops:
  0.0 1.4 %fusion = (bf16[4,64,2048]{2,1,0:T(8,128)(2,1)S(1)}, bf16[4,64,2048]{2,1,0:T(8,128)(2,1)S(1)}) fusion(f32[64,2048]{1,0:T(8,128)} %constant.3, f32[4,2048]{1,0:T(4,128)} %param.4), kind=kLoop, calls=%fused_computation.2 | loop fusion | flops 2621440 | bytes 2654208 | tf_op jit(solution)/shard_map/convert_element_type | solution.py:48
  1.4 51.6 %shard_map.37 = (bf16[8,32,2,16,256]{4,3,2,1,0:T(8,128)(2,1)S(1)}, bf16[2,512,512]{2,1,0:T(8,128)(2,1)S(1)}) custom-call(bf16[4,64,2048]{2,1,0:T(8,128)(2,1)S(1)} %get-tuple-element.10.high_ref, bf16[4,64,2048]{2,1,0:T(8,128)(2,1)S(1)} %get-tuple-element.9.low_ref, bf16[32768,256]{1,0:T(8,128)(2,1)} %volt_ref.1), custom_call_target="tpu_custom_call" | custom-call | tf_op jit(solution)/shard_map/pallas_call | solution.py:302
  53.0 3.8 %shard_map.38 = f32[2,2,256,2048]{3,2,1,0:T(8,128)} custom-call(bf16[2,512,512]{2,1,0:T(8,128)(2,1)S(1)} %get-tuple-element.7.left_ref, bf16[8,32,2,16,256]{4,3,2,1,0:T(8,128)(2,1)S(1)} %get-tuple-element.8.other_ref), custom_call_target="tpu_custom_call" | custom-call | tf_op jit(solution)/shard_map/pallas_call | solution.py:356
